TPU v7x, 32 devices: a whole 2x2x4 slice. The times are simulated.
32 devices in a mesh: slot: 4 (over y, x), seq: 2 (over core), blk: 4 (over z).
Axes of the slice: x: 2, y: 2, z: 4, core: 2. Of those that a mesh axis runs over, the one named last changes fastest.
Arguments:
- tokens: bfloat16 [4, 1024, 2048], P('slot', ('blk', 'seq')), may hold values from -6 to 6
- out_grad: bfloat16 [4, 1024, 2048], P('slot', ('blk', 'seq')), may hold values from -6 to 6
- lengths: int32 [4], P('slot'), may hold values from 256 to 1024, as said below
- attn_gain: bfloat16 [2048], P(('slot', 'blk')), may hold values from 0.099609375 to 1.8984375
- w_query: bfloat16 [2048, 2048], P(('slot', 'blk'), 'seq'), may hold values from -0.125 to 0.125
- w_key: bfloat16 [2048, 2048], P(('slot', 'blk'), 'seq'), may hold values from -0.125 to 0.125
- w_value: bfloat16 [2048, 2048], P(('slot', 'blk'), 'seq'), may hold values from -0.125 to 0.125
- output_weight: bfloat16 [2048, 2048], P(('slot', 'blk'), 'seq'), may hold values from -1 to 1
- mlp_gain: bfloat16 [2048], P(('slot', 'blk')), may hold values from 0.099609375 to 1.8984375
- gate_weight: bfloat16 [2048, 8192], P(('slot', 'blk'), 'seq'), may hold values from -0.125 to 0.125
- up_weight: bfloat16 [2048, 8192], P(('slot', 'blk'), 'seq'), may hold values from -0.125 to 0.125
- down_weight: bfloat16 [2048, 8192], P(('slot', 'blk'), 'seq'), may hold values from -0.0625 to 0.0625
Outputs:
- layer_out: bfloat16 [4, 1024, 2048], P('slot', ('blk', 'seq'))
- grad_tokens: float32 [4, 1024, 2048], P('slot', ('blk', 'seq'))
- grad_attn_gain: float32 [2048], P(('slot', 'blk'))
- grad_w_query: float32 [2048, 2048], P(('slot', 'blk'), 'seq')
- grad_w_key: float32 [2048, 2048], P(('slot', 'blk'), 'seq')
- grad_w_value: float32 [2048, 2048], P(('slot', 'blk'), 'seq')
- grad_w_output: float32 [2048, 2048], P(('slot', 'blk'), 'seq')
- grad_mlp_gain: float32 [2048], P(('slot', 'blk'))
- grad_w_gate: float32 [2048, 8192], P(('slot', 'blk'), 'seq')
- grad_w_up: float32 [2048, 8192], P(('slot', 'blk'), 'seq')
- grad_w_down: float32 [2048, 8192], P(('slot', 'blk'), 'seq')
Inputs may be any that keep to these rules, and one draw needn't show every extreme that they name: `lengths`: the valid tokens of a slot are its first ones; at least one slot is full.
All inputs are finite; a program needn't handle non-finite values.
Results may differ from a plain program's by a relative error of at most 0.025.
Values may be sent and summed in bfloat16 or wider, within the bound.
No kernel may reach another device: no remote copies, remote signals or barrier semaphores. Data moves between devices by JAX's collectives and lax.ppermute only.
A program may use at most 192 MiB of HBM per device.

v0:
```python
from functools import partial
import jax
import jax.numpy as jnp
from jax import lax
from jax.sharding import PartitionSpec as P

HEADS = 32
HEAD_DIM = 64
EPSILON = 1e-05
ROPE_BASE = 130000.0


def from_behind(value, axis, steps):
    count = lax.axis_size(axis)
    first, last = (max(0, -steps), min(count, count - steps))
    return lax.ppermute(value, axis, [(source, source + steps) for source in range(first, last)])


def from_behind_2(array, axis, by):
    peers = lax.axis_size(axis)
    return lax.ppermute(array, axis, [(i, (i + by) % peers) for i in range(peers)])


def rope_tables(positions, head_size):
    half_size = head_size // 2
    frequency = ROPE_BASE ** (-jnp.arange(half_size, dtype=jnp.float32) * 2.0 / head_size)
    angles = positions.astype(jnp.float32)[:, None] * frequency[None, :]
    return (jnp.cos(angles), jnp.sin(angles))


def rotate(vectors, cosine, sine_tab):
    half_size = vectors.shape[-1] // 2
    first_half = vectors[..., :half_size]
    second_half = vectors[..., half_size:]
    cos_wide = cosine[:, None, :]
    sin_wide = sine_tab[:, None, :]
    return jnp.concatenate(
        [
            first_half * cos_wide - second_half * sin_wide,
            second_half * cos_wide + first_half * sin_wide,
        ],
        axis=-1,
    )


def norm_rows(input_rows_packed, gain_row):
    inverse = lax.rsqrt(
        jnp.mean(input_rows_packed * input_rows_packed, axis=-1, keepdims=True) + EPSILON
    )
    return (input_rows_packed * inverse * gain_row, inverse)


def norm_back(input_rows_packed, inverse, gain_row, upstream):
    scaled = upstream * gain_row
    normed = input_rows_packed * inverse
    grad_in = inverse * (scaled - normed * jnp.mean(scaled * normed, axis=-1, keepdims=True))
    return (grad_in, jnp.sum(upstream * normed, axis=0))


def matmul(left, right):
    return jnp.dot(left, right, preferred_element_type=jnp.float32)


def over_rows(left, right):
    return lax.dot_general(
        left, right, (((0,), (0,)), ((), ())), preferred_element_type=jnp.float32
    )


def over_cols(left, right):
    return lax.dot_general(
        left, right, (((1,), (1,)), ((), ())), preferred_element_type=jnp.float32
    )


def block_scores(queries, key_rows, query_pos, key_first, length, score_scale):
    key_pos = key_first + jnp.arange(key_rows.shape[0], dtype=jnp.int32)
    allowed = (key_pos[None, :] <= query_pos[:, None]) & (key_pos[None, :] < length)
    scores = (
        jnp.einsum("qhd,khd->hqk", queries, key_rows, preferred_element_type=jnp.float32)
        * score_scale
    )
    return jnp.where(allowed[None, :, :], scores, -jnp.inf)


def attend_tile(tile_item, key_rows, val_rows, key_first, length, score_scale):
    queries, query_pos, run_max, run_sum, run_out = tile_item
    scores = block_scores(queries, key_rows, query_pos, key_first, length, score_scale)
    new_max = jnp.maximum(run_max, jnp.max(scores, axis=2))
    factor = jnp.exp(run_max - new_max)
    exp_weights = jnp.exp(scores - new_max[:, :, None])
    run_sum = run_sum * factor + jnp.sum(exp_weights, axis=2)
    mixed_out = jnp.einsum(
        "hqk,khd->qhd",
        exp_weights.astype(jnp.bfloat16),
        val_rows,
        preferred_element_type=jnp.float32,
    )
    run_out = run_out * jnp.transpose(factor)[:, :, None] + mixed_out
    return (new_max, run_sum, run_out)


def back_tile(carried, tile_item, key_rows, val_rows, key_first, length, score_scale):
    grad_keys, grad_vals = carried
    queries, query_pos, out_cot, log_sum, row_dot, grad_query = tile_item
    scores = block_scores(queries, key_rows, query_pos, key_first, length, score_scale)
    probs = jnp.exp(scores - log_sum[:, :, None])
    grad_vals = grad_vals + jnp.einsum(
        "hqk,qhd->khd", probs.astype(jnp.bfloat16), out_cot, preferred_element_type=jnp.float32
    )
    grad_weight = jnp.einsum("qhd,khd->hqk", out_cot, val_rows, preferred_element_type=jnp.float32)
    grad_scores = (probs * (grad_weight - row_dot[:, :, None])).astype(jnp.bfloat16)
    grad_query = (
        grad_query
        + jnp.einsum("hqk,khd->qhd", grad_scores, key_rows, preferred_element_type=jnp.float32)
        * score_scale
    )
    grad_keys = (
        grad_keys
        + jnp.einsum("hqk,qhd->khd", grad_scores, queries, preferred_element_type=jnp.float32)
        * score_scale
    )
    return ((grad_keys, grad_vals), grad_query)


def sum_mlp(term_gate, term_up, term_down):
    return (
        lax.psum_scatter(
            term_gate.astype(jnp.bfloat16), ("slot", "blk"), scatter_dimension=0, tiled=True
        ).astype(jnp.float32),
        lax.psum_scatter(
            term_up.astype(jnp.bfloat16), ("slot", "blk"), scatter_dimension=0, tiled=True
        ).astype(jnp.float32),
        lax.psum_scatter(
            term_down.astype(jnp.bfloat16), ("slot", "blk"), scatter_dimension=0, tiled=True
        ).astype(jnp.float32),
    )


def shards(
    tokens,
    out_grad,
    lengths,
    attn_gain,
    w_query,
    w_key,
    w_value,
    output_weight,
    mlp_gain,
    gate_weight,
    up_weight,
    down_weight,
):
    seq_count = lax.axis_size("seq")
    blk_count = lax.axis_size("blk")
    seq_rank = lax.axis_index("seq")
    blk_rank = lax.axis_index("blk")
    tok_rows = tokens.shape[1]
    block_len = tok_rows * seq_count
    local_heads = HEADS // seq_count
    local_width = local_heads * HEAD_DIM
    score_scale = HEAD_DIM ** (-0.5)
    length = lengths[0]
    block_pos = blk_rank * block_len + jnp.arange(block_len, dtype=jnp.int32)
    positions = blk_rank * block_len + seq_rank * tok_rows + jnp.arange(tok_rows, dtype=jnp.int32)
    live_rows = (positions < length)[:, None]
    input_rows_packed = tokens[0].astype(jnp.float32)
    cosine, sine_tab = rope_tables(block_pos, HEAD_DIM)
    head_shape = (block_len, local_heads, HEAD_DIM)
    tile_rows = min(512, block_len)
    tile_count = block_len // tile_rows
    tiled_shape = (tile_count, tile_rows, local_heads, HEAD_DIM)
    pos_tiles = block_pos.reshape(tile_count, tile_rows)
    (
        gain_attn,
        gain_mlp,
        full_query,
        full_key,
        full_value,
        full_output,
        full_gate,
        full_up,
        full_down,
    ) = (
        lax.all_gather(attn_gain, ("slot", "blk"), axis=0, tiled=True),
        lax.all_gather(mlp_gain, ("slot", "blk"), axis=0, tiled=True),
        lax.all_gather(w_query, ("slot", "blk"), axis=0, tiled=True),
        lax.all_gather(w_key, ("slot", "blk"), axis=0, tiled=True),
        lax.all_gather(w_value, ("slot", "blk"), axis=0, tiled=True),
        lax.all_gather(output_weight, ("slot", "blk"), axis=0, tiled=True),
        lax.all_gather(gate_weight, ("slot", "blk"), axis=0, tiled=True),
        lax.all_gather(up_weight, ("slot", "blk"), axis=0, tiled=True),
        lax.all_gather(down_weight, ("slot", "blk"), axis=0, tiled=True),
    )
    gain_attn_f = gain_attn.astype(jnp.float32)
    gain_mlp_f = gain_mlp.astype(jnp.float32)
    normed_attn, inverse_attn = norm_rows(input_rows_packed, gain_attn_f)
    hidden_after_attention = normed_attn.astype(jnp.bfloat16)
    hidden_block = lax.all_gather(hidden_after_attention, "seq", axis=0, tiled=True)
    queries = rotate(matmul(hidden_block, full_query).reshape(head_shape), cosine, sine_tab).astype(
        jnp.bfloat16
    )
    key_rows = rotate(matmul(hidden_block, full_key).reshape(head_shape), cosine, sine_tab).astype(
        jnp.bfloat16
    )
    val_rows = matmul(hidden_block, full_value).astype(jnp.bfloat16).reshape(head_shape)
    query_tiles = queries.reshape(tiled_shape)
    run_max = jnp.full((tile_count, local_heads, tile_rows), -1e30, jnp.float32)
    run_sum = jnp.zeros((tile_count, local_heads, tile_rows), jnp.float32)
    run_out = jnp.zeros(tiled_shape, jnp.float32)
    kept_blocks = []
    moving_keys, moving_vals = (key_rows, val_rows)
    for cycle_step in range(blk_count):
        key_first = (blk_rank - cycle_step) % blk_count * block_len
        kept_blocks.append((moving_keys, moving_vals, key_first))
        step_fn = partial(
            attend_tile,
            key_rows=moving_keys,
            val_rows=moving_vals,
            key_first=key_first,
            length=length,
            score_scale=score_scale,
        )
        run_max, run_sum, run_out = lax.map(
            step_fn, (query_tiles, pos_tiles, run_max, run_sum, run_out)
        )
        if cycle_step + 1 < blk_count:
            moving_keys, moving_vals = from_behind((moving_keys, moving_vals), "blk", 1)
    log_sum = run_max + jnp.log(run_sum)
    attended_tiles = (run_out / jnp.transpose(run_sum, (0, 2, 1))[:, :, :, None]).astype(
        jnp.bfloat16
    )
    attention_mixed = attended_tiles.reshape(block_len, local_width)
    residual_stream = input_rows_packed + lax.psum_scatter(
        over_cols(attention_mixed, full_output).astype(jnp.bfloat16),
        "seq",
        scatter_dimension=0,
        tiled=True,
    ).astype(jnp.float32)
    normed_mlp, inverse_mlp = norm_rows(residual_stream, gain_mlp_f)
    hidden_after_feedforward = normed_mlp.astype(jnp.bfloat16)
    mlp_block = lax.all_gather(hidden_after_feedforward, "seq", axis=0, tiled=True)
    gate_logits = matmul(mlp_block, full_gate)
    up_logits = matmul(mlp_block, full_up)
    sigmoid_gate = jax.nn.sigmoid(gate_logits)
    swiglu_product = (gate_logits * sigmoid_gate * up_logits).astype(jnp.bfloat16)
    mlp_proj = lax.psum_scatter(
        over_cols(swiglu_product, full_down).astype(jnp.bfloat16),
        "seq",
        scatter_dimension=0,
        tiled=True,
    ).astype(jnp.float32)
    block_out = jnp.where(live_rows, residual_stream + mlp_proj, 0.0)
    out_cot = jnp.where(live_rows, out_grad[0].astype(jnp.float32), 0.0)
    cot_block = lax.all_gather(out_cot.astype(jnp.bfloat16), "seq", axis=0, tiled=True)
    grad_down_term = over_rows(cot_block, swiglu_product)
    grad_act = matmul(cot_block, full_down)
    grad_gate = (
        grad_act * up_logits * sigmoid_gate * (1.0 + gate_logits * (1.0 - sigmoid_gate))
    ).astype(jnp.bfloat16)
    grad_up = (grad_act * gate_logits * sigmoid_gate).astype(jnp.bfloat16)
    grad_gate_term = over_rows(mlp_block, grad_gate)
    grad_up_term = over_rows(mlp_block, grad_up)
    grad_hidden_mlp = lax.psum_scatter(
        (over_cols(grad_gate, full_gate) + over_cols(grad_up, full_up)).astype(jnp.bfloat16),
        "seq",
        scatter_dimension=0,
        tiled=True,
    ).astype(jnp.float32)
    grad_resid_part, gain_mlp_term = norm_back(
        residual_stream, inverse_mlp, gain_mlp_f, grad_hidden_mlp
    )
    grad_resid = out_cot + grad_resid_part
    resid_block = lax.all_gather(grad_resid.astype(jnp.bfloat16), "seq", axis=0, tiled=True)
    grad_wout_term = over_rows(resid_block, attention_mixed)
    grad_attended = matmul(resid_block, full_output).astype(jnp.bfloat16)
    cot_tiles = grad_attended.reshape(tiled_shape)
    row_dot = jnp.transpose(
        jnp.sum(cot_tiles.astype(jnp.float32) * attended_tiles.astype(jnp.float32), axis=-1),
        (0, 2, 1),
    )
    grad_query = jnp.zeros(tiled_shape, jnp.float32)
    moving_grads = (jnp.zeros(head_shape, jnp.float32), jnp.zeros(head_shape, jnp.float32))
    for kept_keys, kept_vals, key_first in kept_blocks:
        back_fn = partial(
            back_tile,
            key_rows=kept_keys,
            val_rows=kept_vals,
            key_first=key_first,
            length=length,
            score_scale=score_scale,
        )
        moving_grads, grad_query = lax.scan(
            back_fn, moving_grads, (query_tiles, pos_tiles, cot_tiles, log_sum, row_dot, grad_query)
        )
        moving_grads = (
            from_behind_2(moving_grads[0].astype(jnp.bfloat16), "blk", 1).astype(jnp.float32),
            from_behind_2(moving_grads[1].astype(jnp.bfloat16), "blk", 1).astype(jnp.float32),
        )
    grad_keys, grad_vals = moving_grads
    grad_query_low = grad_query.reshape(head_shape).astype(jnp.bfloat16).astype(jnp.float32)
    grad_keys_low = grad_keys.astype(jnp.bfloat16).astype(jnp.float32)
    grad_query_pre = (
        rotate(grad_query_low, cosine, -sine_tab)
        .astype(jnp.bfloat16)
        .reshape(block_len, local_width)
    )
    grad_key_pre = (
        rotate(grad_keys_low, cosine, -sine_tab)
        .astype(jnp.bfloat16)
        .reshape(block_len, local_width)
    )
    grad_value_low = grad_vals.astype(jnp.bfloat16).reshape(block_len, local_width)
    grad_hidden_attn = lax.psum_scatter(
        (
            over_cols(grad_query_pre, full_query)
            + over_cols(grad_key_pre, full_key)
            + over_cols(grad_value_low, full_value)
        ).astype(jnp.bfloat16),
        "seq",
        scatter_dimension=0,
        tiled=True,
    ).astype(jnp.float32)
    grad_in_part, gain_attn_term = norm_back(
        input_rows_packed, inverse_attn, gain_attn_f, grad_hidden_attn
    )
    grad_wgate, grad_wup, grad_wdown = sum_mlp(grad_gate_term, grad_up_term, grad_down_term)
    grad_wquery, grad_wkey, grad_wvalue, grad_woutput, gain_attn_part, gain_mlp_part = (
        lax.psum_scatter(
            over_rows(hidden_block, grad_query_pre).astype(jnp.bfloat16),
            ("slot", "blk"),
            scatter_dimension=0,
            tiled=True,
        ).astype(jnp.float32),
        lax.psum_scatter(
            over_rows(hidden_block, grad_key_pre).astype(jnp.bfloat16),
            ("slot", "blk"),
            scatter_dimension=0,
            tiled=True,
        ).astype(jnp.float32),
        lax.psum_scatter(
            over_rows(hidden_block, grad_value_low).astype(jnp.bfloat16),
            ("slot", "blk"),
            scatter_dimension=0,
            tiled=True,
        ).astype(jnp.float32),
        lax.psum_scatter(
            grad_wout_term.astype(jnp.bfloat16), ("slot", "blk"), scatter_dimension=0, tiled=True
        ).astype(jnp.float32),
        lax.psum_scatter(
            gain_attn_term.astype(jnp.bfloat16), ("slot", "blk"), scatter_dimension=0, tiled=True
        ).astype(jnp.float32),
        lax.psum_scatter(
            gain_mlp_term.astype(jnp.bfloat16), ("slot", "blk"), scatter_dimension=0, tiled=True
        ).astype(jnp.float32),
    )
    grad_gattn, grad_gmlp = lax.psum((gain_attn_part, gain_mlp_part), "seq")
    grad_inputs = grad_resid + grad_in_part
    return (
        block_out.astype(jnp.bfloat16)[None],
        grad_inputs[None],
        grad_gattn,
        grad_wquery,
        grad_wkey,
        grad_wvalue,
        grad_woutput,
        grad_gmlp,
        grad_wgate,
        grad_wup,
        grad_wdown,
    )


def solution(mesh):
    placed = (
        P("slot", ("blk", "seq"), None),
        P("slot", ("blk", "seq"), None),
        P("slot"),
        P(("slot", "blk")),
        P(("slot", "blk"), "seq"),
        P(("slot", "blk"), "seq"),
        P(("slot", "blk"), "seq"),
        P(("slot", "blk"), "seq"),
        P(("slot", "blk")),
        P(("slot", "blk"), "seq"),
        P(("slot", "blk"), "seq"),
        P(("slot", "blk"), "seq"),
    )
    return jax.shard_map(
        shards,
        mesh=mesh,
        in_specs=placed,
        out_specs=(
            P("slot", ("blk", "seq"), None),
            P("slot", ("blk", "seq"), None),
            P(("slot", "blk")),
            P(("slot", "blk"), "seq"),
            P(("slot", "blk"), "seq"),
            P(("slot", "blk"), "seq"),
            P(("slot", "blk"), "seq"),
            P(("slot", "blk")),
            P(("slot", "blk"), "seq"),
            P(("slot", "blk"), "seq"),
            P(("slot", "blk"), "seq"),
        ),
        check_vma=False,
    )
```

profile of v0, /device:TPU:0, one launch (start us, length us, event | category | flops | bytes accessed | tf_op | source)
XLA Modules:
  0.0 2703.3 jit_solution(6175386488568458087)
XLA Ops:
  8.5 42.4 %all-gather = bf16[16,1,128]{2,1,0:T(2,128)(2,1)S(1)} all-gather(bf16[1,1,128]{2,1,0:T(2,128)(2,1)} %bitcast.279), channel_id=1, replica_groups=mesh['slot'=4,'seq'=2,'blk'=4] {'slot','blk'}, dimensions={0}, use_global_device_ids=true | all-gather | bytes 4352 | tf_op jit(solution)/shard_map/all_gather | solution.py:185
  58.4 79.9 %all-gather.18.cloned.1.call-done = bf16[2048,1024]{1,0:T(8,128)(2,1)} async-done(((bf16[128,1024]{1,0:T(8,128)(2,1)}), bf16[2048,1024]{1,0:T(8,128)(2,1)}) %all-gather.18.cloned.1.call-update) | async-done | bytes 4194320 | tf_op jit(solution)/shard_map/all_gather | solution.py:188
  142.5 73.0 %all-gather.16.cloned.1.call-done = bf16[2048,1024]{1,0:T(8,128)(2,1)} async-done(((bf16[128,1024]{1,0:T(8,128)(2,1)}), bf16[2048,1024]{1,0:T(8,128)(2,1)}) %all-gather.16.cloned.1.call-update) | async-done | bytes 4194320 | tf_op jit(solution)/shard_map/all_gather | solution.py:187
  223.3 71.0 %all-gather.20.cloned.1.call-done = bf16[2048,1024]{1,0:T(8,128)(2,1)} async-done(((bf16[128,1024]{1,0:T(8,128)(2,1)}), bf16[2048,1024]{1,0:T(8,128)(2,1)}) %all-gather.20.cloned.1.call-update) | async-done | bytes 4194320 | tf_op jit(solution)/shard_map/all_gather | solution.py:189
  307.3 14.4 collective-permute-done.1
  326.9 15.0 collective-permute-done.2
  364.6 16.0 collective-permute-done.4
  405.8 40.4 %all-gather.1 = bf16[16,1,128]{2,1,0:T(2,128)(2,1)S(1)} all-gather(bf16[1,1,128]{2,1,0:T(2,128)(2,1)S(1)} %bitcast.280), channel_id=1, replica_groups=mesh['slot'=4,'seq'=2,'blk'=4] {'slot','blk'}, dimensions={0}, use_global_device_ids=true | all-gather | bytes 4352 | tf_op jit(solution)/shard_map/all_gather | solution.py:186
  456.0 195.9 %all-gather.28.cloned.1.call-done = bf16[2048,4096]{1,0:T(8,128)(2,1)} async-done(((bf16[128,4096]{1,0:T(8,128)(2,1)}), bf16[2048,4096]{1,0:T(8,128)(2,1)}) %all-gather.28.cloned.1.call-update) | async-done | bytes 16777232 | tf_op jit(solution)/shard_map/all_gather | solution.py:192
  652.0 12.6 fusion.191
  664.6 180.3 %all-gather.26.cloned.1.call-done = bf16[2048,4096]{1,0:T(8,128)(2,1)} async-done(((bf16[128,4096]{1,0:T(8,128)(2,1)}), bf16[2048,4096]{1,0:T(8,128)(2,1)}) %all-gather.26.cloned.1.call-update) | async-done | bytes 16777232 | tf_op jit(solution)/shard_map/all_gather | solution.py:191
  855.1 195.1 %all-gather.30.cloned.1.call-done = bf16[2048,4096]{1,0:T(8,128)(2,1)} async-done(((bf16[128,4096]{1,0:T(8,128)(2,1)}), bf16[2048,4096]{1,0:T(8,128)(2,1)}) %all-gather.30.cloned.1.call-update) | async-done | bytes 16777232 | tf_op jit(solution)/shard_map/all_gather | solution.py:193
  1050.2 13.4 multiply_convert_fusion.4
  1063.6 12.3 fusion.192
  1075.9 12.5 fusion.12
  1180.1 11.0 collective-permute-done.8
  1227.4 12.3 convolution_convert_fusion.7
  1292.5 44.2 %all-reduce.3 = (bf16[2048]{0:T(1024)(128)(2,1)S(1)}, bf16[2048]{0:T(1024)(128)(2,1)S(1)}) all-reduce(bf16[2048]{0:T(1024)(128)(2,1)S(1)} %get-tuple-element.228, bf16[2048]{0:T(1024)(128)(2,1)S(1)} %copy-done.53), channel_id=6, replica_groups=mesh['slot'=4,'seq'=2,'blk'=4] {'slot','blk'}, use_global_device_ids=true, to_apply=%region_18.19.clone | all-reduce | flops 4096 | bytes 16384
  1351.5 95.0 %reduce-scatter.24.cloned.1.call-done = bf16[128,1024]{1,0:T(8,128)(2,1)} async-done(((bf16[2048,1024]{1,0:T(8,128)(2,1)}), bf16[128,1024]{1,0:T(8,128)(2,1)}) %reduce-scatter.24.cloned.1.call-update) | async-done | bytes 262160 | tf_op jit(solution)/shard_map/reduce_scatter | solution.py:341
  1448.3 95.0 %reduce-scatter.22.cloned.1.call-done = bf16[128,1024]{1,0:T(8,128)(2,1)} async-done(((bf16[2048,1024]{1,0:T(8,128)(2,1)}), bf16[128,1024]{1,0:T(8,128)(2,1)}) %reduce-scatter.22.cloned.1.call-update) | async-done | bytes 262160 | tf_op jit(solution)/shard_map/reduce_scatter | solution.py:335
  1545.2 95.2 %reduce-scatter.20.cloned.1.call-done = bf16[128,1024]{1,0:T(8,128)(2,1)} async-done(((bf16[2048,1024]{1,0:T(8,128)(2,1)}), bf16[128,1024]{1,0:T(8,128)(2,1)}) %reduce-scatter.20.cloned.1.call-update) | async-done | bytes 262160 | tf_op jit(solution)/shard_map/reduce_scatter | solution.py:329
  1642.1 348.7 %reduce-scatter.30.cloned.1.call-done = bf16[128,4096]{1,0:T(8,128)(2,1)} async-done(((bf16[2048,4096]{1,0:T(8,128)(2,1)}), bf16[128,4096]{1,0:T(8,128)(2,1)}) %reduce-scatter.30.cloned.1.call-update) | async-done | bytes 1048592 | tf_op jit(solution)/shard_map/reduce_scatter | solution.py:131
  1993.6 348.6 %reduce-scatter.28.cloned.1.call-done = bf16[128,4096]{1,0:T(8,128)(2,1)} async-done(((bf16[2048,4096]{1,0:T(8,128)(2,1)}), bf16[128,4096]{1,0:T(8,128)(2,1)}) %reduce-scatter.28.cloned.1.call-update) | async-done | bytes 1048592 | tf_op jit(solution)/shard_map/reduce_scatter | solution.py:128
  2344.9 348.6 %reduce-scatter.32.cloned.1.call-done = bf16[128,4096]{1,0:T(8,128)(2,1)} async-done(((bf16[2048,4096]{1,0:T(8,128)(2,1)}), bf16[128,4096]{1,0:T(8,128)(2,1)}) %reduce-scatter.32.cloned.1.call-update) | async-done | bytes 1048592 | tf_op jit(solution)/shard_map/reduce_scatter | solution.py:134
  (312 shorter events, 313.4 us)
Async XLA Ops:
  7.2 51.2 %all-gather.14.cloned.1.call-start = ((), (), s32[]{:S(2)}) async-start(), calls=%async_computation.11 | async-start | bytes 1572864 | tf_op jit(solution)/shard_map/all_gather | solution.py:199
  52.9 85.3 %all-gather.18.cloned.1.call-start = ((), (), s32[]{:S(2)}) async-start(), calls=%async_computation.13 | async-start | bytes 4456448 | tf_op jit(solution)/shard_map/all_gather | solution.py:188
  53.7 161.9 %all-gather.16.cloned.1.call-start = ((), (), s32[]{:S(2)}) async-start(), calls=%async_computation.12 | async-start | bytes 4456448 | tf_op jit(solution)/shard_map/all_gather | solution.py:187
  54.4 239.9 %all-gather.20.cloned.1.call-start = ((), (), s32[]{:S(2)}) async-start(), calls=%async_computation.14 | async-start | bytes 4456448 | tf_op jit(solution)/shard_map/all_gather | solution.py:189
  55.0 345.5 %all-gather.22.cloned.1.call-start = ((), (), s32[]{:S(2)}) async-start(), calls=%async_computation.15 | async-start | bytes 4456448 | tf_op jit(solution)/shard_map/all_gather | solution.py:190
  55.6 390.7 %reduce-scatter.12.cloned.1.call-start = ((), (), s32[]{:S(2)}) async-start(), calls=%async_computation.16 | async-start | bytes 1572864 | tf_op jit(solution)/shard_map/reduce_scatter | solution.py:234
  219.9 84.1 %collective-permute-start = (bf16[256,16,64]{0,2,1:T(8,128)(2,1)S(1)}, bf16[256,16,64]{0,2,1:T(8,128)(2,1)S(1)}, u32[]{:S(2)}, u32[]{:S(2)}) collective-permute-start(bf16[256,16,64]{0,2,1:T(8,128)(2,1)S(1)} %pad_maximum_fusion.1), channel_id=1, source_target_pairs={{0,1},{1,2},{2,3},{4,5},{5,6},{6,7},{8,9},{9,10},{10,11},{12,13},{... | collective-permute-start | bytes 1572872 | tf_op jit(solution)/shard_map/ppermute | solution.py:16
  341.9 38.7 %collective-permute-start.4 = (bf16[256,16,64]{0,2,1:T(8,128)(2,1)S(1)}, bf16[256,16,64]{0,2,1:T(8,128)(2,1)S(1)}, u32[]{:S(2)}, u32[]{:S(2)}) collective-permute-start(bf16[256,16,64]{0,2,1:T(8,128)(2,1)S(1)} %collective-permute-done.2), channel_id=1, source_target_pairs={{0,1},{1,2},{2,3},{4,5},{5,6},{6,7},{8,9},{9,10},{10,11},{12,13},{... | collective-permute-start | bytes 1572872 | tf_op jit(solution)/shard_map/ppermute | solution.py:16
  358.2 40.3 %collective-permute-start.5 = (bf16[256,16,64]{0,2,1:T(8,128)(2,1)S(1)}, bf16[256,16,64]{0,2,1:T(8,128)(2,1)S(1)}, u32[]{:S(2)}, u32[]{:S(2)}) collective-permute-start(bf16[256,16,64]{0,2,1:T(8,128)(2,1)S(1)} %collective-permute-done.3), channel_id=1, source_target_pairs={{0,1},{1,2},{2,3},{4,5},{5,6},{6,7},{8,9},{9,10},{10,11},{12,13},{... | collective-permute-start | bytes 1572872 | tf_op jit(solution)/shard_map/ppermute | solution.py:16
  405.7 50.3 %all-gather.24.cloned.1.call-start = ((), (), s32[]{:S(2)}) async-start(), calls=%async_computation.17 | async-start | bytes 1572864 | tf_op jit(solution)/shard_map/all_gather | solution.py:242
  449.6 202.3 %all-gather.28.cloned.1.call-start = ((), (), s32[]{:S(2)}) async-start(), calls=%async_computation.19 | async-start | bytes 17825792 | tf_op jit(solution)/shard_map/all_gather | solution.py:192
  450.4 394.6 %all-gather.26.cloned.1.call-start = ((), (), s32[]{:S(2)}) async-start(), calls=%async_computation.18 | async-start | bytes 17825792 | tf_op jit(solution)/shard_map/all_gather | solution.py:191
  451.1 404.0 %all-gather.32.cloned.1.call-start = ((), (), s32[]{:S(2)}) async-start(), calls=%async_computation.22 | async-start | bytes 1572864 | tf_op jit(solution)/shard_map/all_gather | solution.py:255
  452.2 598.0 %all-gather.30.cloned.1.call-start = ((), (), s32[]{:S(2)}) async-start(), calls=%async_computation.20 | async-start | bytes 17825792 | tf_op jit(solution)/shard_map/all_gather | solution.py:193
  452.9 642.4 %reduce-scatter.16.cloned.1.call-start = ((), (), s32[]{:S(2)}) async-start(), calls=%async_computation.23 | async-start | bytes 1572864 | tf_op jit(solution)/shard_map/reduce_scatter | solution.py:264
  1100.3 190.6 %reduce-scatter.18.cloned.1.call-start = ((), (), s32[]{:S(2)}) async-start(), calls=%async_computation.25 | async-start | bytes 1572864 | tf_op jit(solution)/shard_map/reduce_scatter | solution.py:314
  1227.4 112.4 %reduce-scatter.14.cloned.1.call-start = ((), (), s32[]{:S(2)}) async-start(), calls=%async_computation.21 | async-start | bytes 1572864 | tf_op jit(solution)/shard_map/reduce_scatter | solution.py:247
  1239.7 110.0 %reduce-scatter.26.cloned.1.call-start = ((), (), s32[]{:S(2)}) async-start(), calls=%async_computation.29 | async-start | bytes 4456448 | tf_op jit(solution)/shard_map/reduce_scatter | solution.py:347
  1244.7 201.8 %reduce-scatter.24.cloned.1.call-start = ((), (), s32[]{:S(2)}) async-start(), calls=%async_computation.28 | async-start | bytes 4456448 | tf_op jit(solution)/shard_map/reduce_scatter | solution.py:341
  1249.1 294.2 %reduce-scatter.22.cloned.1.call-start = ((), (), s32[]{:S(2)}) async-start(), calls=%async_computation.27 | async-start | bytes 4456448 | tf_op jit(solution)/shard_map/reduce_scatter | solution.py:335
  1252.6 387.7 %reduce-scatter.20.cloned.1.call-start = ((), (), s32[]{:S(2)}) async-start(), calls=%async_computation.26 | async-start | bytes 4456448 | tf_op jit(solution)/shard_map/reduce_scatter | solution.py:329
  1256.9 733.9 %reduce-scatter.30.cloned.1.call-start = ((), (), s32[]{:S(2)}) async-start(), calls=%async_computation.31 | async-start | bytes 17825792 | tf_op jit(solution)/shard_map/reduce_scatter | solution.py:131
  1268.0 1074.2 %reduce-scatter.28.cloned.1.call-start = ((), (), s32[]{:S(2)}) async-start(), calls=%async_computation.30 | async-start | bytes 17825792 | tf_op jit(solution)/shard_map/reduce_scatter | solution.py:128
  1277.9 1415.5 %reduce-scatter.32.cloned.1.call-start = ((), (), s32[]{:S(2)}) async-start(), calls=%async_computation.32 | async-start | bytes 17825792 | tf_op jit(solution)/shard_map/reduce_scatter | solution.py:134
  (81 other events, 2319.7 us)
Sparse Core Ops, SparseCore 0:
  53.0 5.3 all-gather.13
  61.1 77.0 all-gather.17
  141.0 74.4 all-gather.15
  218.1 76.0 all-gather.19
  296.9 100.4 all-gather.21
  405.9 9.3 reduce-scatter.11
  449.8 6.2 all-gather.23
  459.2 192.7 all-gather.27
  655.1 189.7 all-gather.25
  847.0 7.2 all-gather.31
  857.4 192.7 all-gather.29
  1088.6 6.7 reduce-scatter.15
  1100.4 10.1 all-gather.33
  1227.5 7.8 reduce-scatter.17
  1239.8 7.5 reduce-scatter.13
  1249.5 100.1 reduce-scatter.25
  1351.9 94.6 reduce-scatter.23
  1448.7 94.6 reduce-scatter.21
  1545.7 94.6 reduce-scatter.19
  1642.5 348.3 reduce-scatter.29
  1993.1 348.9 reduce-scatter.27
  2344.4 348.9 reduce-scatter.31
where the time goes:
time: 2710 us; the launch traced here: 2700 us
  waiting for transfers between devices  2300 us (85%)
  matrix products  172 us (6%)
  blocking collectives  130 us (5%)
  other arithmetic  41.5 us (2%)
  starting transfers between devices  30.1 us (1%)
    reduce_scatter x1, waiting for transfers between devices, sum_mlp(): lax.psum_scatter(term_up.astype(jnp.bfloat16), ('slot', 'blk'), scatter_d...  349 us
    reduce_scatter x1, waiting for transfers between devices, sum_mlp(): lax.psum_scatter(term_down.astype(jnp.bfloat16), ('slot', 'blk'), scatter...  349 us
    reduce_scatter x1, waiting for transfers between devices, sum_mlp(): lax.psum_scatter(term_gate.astype(jnp.bfloat16), ('slot', 'blk'), scatter...  349 us
    all_gather x1, waiting for transfers between devices, shards(): lax.all_gather(up_weight, ('slot', 'blk'), axis=0, tiled=True)  196 us
    all_gather x1, waiting for transfers between devices, shards(): lax.all_gather(down_weight, ('slot', 'blk'), axis=0, tiled=True)  195 us
    all_gather x1, waiting for transfers between devices, shards(): lax.all_gather(gate_weight, ('slot', 'blk'), axis=0, tiled=True)  180 us
    reduce_scatter x1, waiting for transfers between devices, shards(): lax.psum_scatter(over_rows(hidden_block, grad_query_pre).astype(jnp.bfloa...  95.2 us
    reduce_scatter x1, waiting for transfers between devices, shards(): lax.psum_scatter(over_rows(hidden_block, grad_key_pre).astype(jnp.bfloat1...  95 us
  transfers between devices with their start and end apart: 36, of which 30 were waited for; matrix products, arithmetic and copies ran while one was open for 5% of the time, Pallas kernels for 0%

commit v1 on v0

--- a/solution.py
+++ b/solution.py
@@ -8,6 +8,16 @@
 HEAD_DIM = 64
 EPSILON = 1e-05
 ROPE_BASE = 130000.0
+
+
+def ring_gather(x, axis, dim):
+    ways, here, hop = (lax.axis_size(axis), lax.axis_index(axis), x.shape[dim])
+    lengths = [n * ways if d == dim else n for d, n in enumerate(x.shape)]
+    full = lax.dynamic_update_slice_in_dim(jnp.zeros(lengths, x.dtype), x, here * hop, axis=dim)
+    for far in range(1, ways):
+        x = lax.ppermute(x, axis, [(d, (d + 1) % ways) for d in range(ways)])
+        full = lax.dynamic_update_slice_in_dim(full, x, (here - far) % ways * hop, axis=dim)
+    return full
 
 
 def from_behind(value, axis, steps):
@@ -188,7 +198,7 @@
         lax.all_gather(w_key, ("slot", "blk"), axis=0, tiled=True),
         lax.all_gather(w_value, ("slot", "blk"), axis=0, tiled=True),
         lax.all_gather(output_weight, ("slot", "blk"), axis=0, tiled=True),
-        lax.all_gather(gate_weight, ("slot", "blk"), axis=0, tiled=True),
+        ring_gather(gate_weight, ("slot", "blk"), 0),
         lax.all_gather(up_weight, ("slot", "blk"), axis=0, tiled=True),
         lax.all_gather(down_weight, ("slot", "blk"), axis=0, tiled=True),
     )

time: 2710 us -> 2810 us (1.037)
  waiting for transfers between devices: 2300 us -> 2340 us
  local copies, waits for them, and re-layouts: 14.2 us -> 48.9 us
    ppermute x0 -> x15, waiting for transfers between devices: none -> 613 us  [ring_gather(): x = lax.ppermute(x, axis, [(d, (d + 1) % ways) for d in range(ways)])]
    all_gather x1, waiting for transfers between devices: 196 us -> 0.01 us  [shards(): lax.all_gather(up_weight, ('slot', 'blk'), axis=0, tiled=True)]
    all_gather x1, waiting for transfers between devices: 195 us -> 0.01 us  [shards(): lax.all_gather(down_weight, ('slot', 'blk'), axis=0, tiled=True)]
    all_gather x1 -> x0, waiting for transfers between devices: 180 us -> none  [shards(): lax.all_gather(gate_weight, ('slot', 'blk'), axis=0, tiled=True)]
  transfers between devices with their start and end apart: 36 -> 50, of which waited for: 30 -> 40; matrix products, arithmetic and copies ran while one was open for 5% -> 6% of each run, Pallas kernels for 0% -> 0%
where the time goes in v1:
time: 2810 us; the launch traced here: 2800 us
  waiting for transfers between devices  2340 us (83%)
  matrix products  169 us (6%)
  blocking collectives  128 us (5%)
  starting transfers between devices  54.4 us (2%)
  local copies, waits for them, and re-layouts  48.9 us (2%)
  other arithmetic  40.2 us (1%)
    ppermute x15, waiting for transfers between devices, ring_gather(): x = lax.ppermute(x, axis, [(d, (d + 1) % ways) for d in range(ways)])  613 us
    reduce_scatter x1, waiting for transfers between devices, sum_mlp(): lax.psum_scatter(term_gate.astype(jnp.bfloat16), ('slot', 'blk'), scatter...  349 us
    reduce_scatter x1, waiting for transfers between devices, sum_mlp(): lax.psum_scatter(term_down.astype(jnp.bfloat16), ('slot', 'blk'), scatter...  349 us
    reduce_scatter x1, waiting for transfers between devices, sum_mlp(): lax.psum_scatter(term_up.astype(jnp.bfloat16), ('slot', 'blk'), scatter_d...  348 us
    reduce_scatter x1, waiting for transfers between devices, shards(): lax.psum_scatter(over_rows(hidden_block, grad_value_low).astype(jnp.bfloa...  95 us
    reduce_scatter x1, waiting for transfers between devices, shards(): lax.psum_scatter(over_rows(hidden_block, grad_query_pre).astype(jnp.bfloa...  95 us
    reduce_scatter x1, waiting for transfers between devices, shards(): lax.psum_scatter(over_rows(hidden_block, grad_key_pre).astype(jnp.bfloat1...  95 us
    all_gather x1, waiting for transfers between devices, shards(): lax.all_gather(w_query, ('slot', 'blk'), axis=0, tiled=True)  79.9 us
  transfers between devices with their start and end apart: 50, of which 40 were waited for; matrix products, arithmetic and copies ran while one was open for 6% of the time, Pallas kernels for 0%

profile of v1, /device:TPU:0, one launch (start us, length us, event | category | flops | bytes accessed | tf_op | source)
XLA Modules:
  0.0 2801.2 jit_solution(16790176681354446307)
XLA Ops:
  7.2 42.4 %all-gather = bf16[16,1,128]{2,1,0:T(2,128)(2,1)S(1)} all-gather(bf16[1,1,128]{2,1,0:T(2,128)(2,1)} %bitcast.279), channel_id=1, replica_groups=mesh['slot'=4,'seq'=2,'blk'=4] {'slot','blk'}, dimensions={0}, use_global_device_ids=true | all-gather | bytes 4352 | tf_op jit(solution)/shard_map/all_gather | solution.py:195
  58.4 79.9 %all-gather.15.cloned.1.call-done = bf16[2048,1024]{1,0:T(8,128)(2,1)} async-done(((bf16[128,1024]{1,0:T(8,128)(2,1)}), bf16[2048,1024]{1,0:T(8,128)(2,1)}) %all-gather.15.cloned.1.call-update) | async-done | bytes 4194320 | tf_op jit(solution)/shard_map/all_gather | solution.py:197
  142.5 73.0 %all-gather.17.cloned.1.call-done = bf16[2048,1024]{1,0:T(8,128)(2,1)} async-done(((bf16[128,1024]{1,0:T(8,128)(2,1)}), bf16[2048,1024]{1,0:T(8,128)(2,1)}) %all-gather.17.cloned.1.call-update) | async-done | bytes 4194320 | tf_op jit(solution)/shard_map/all_gather | solution.py:198
  223.3 71.0 %all-gather.19.cloned.1.call-done = bf16[2048,1024]{1,0:T(8,128)(2,1)} async-done(((bf16[128,1024]{1,0:T(8,128)(2,1)}), bf16[2048,1024]{1,0:T(8,128)(2,1)}) %all-gather.19.cloned.1.call-update) | async-done | bytes 4194320 | tf_op jit(solution)/shard_map/all_gather | solution.py:199
  405.8 40.4 %all-gather.1 = bf16[16,1,128]{2,1,0:T(2,128)(2,1)S(1)} all-gather(bf16[1,1,128]{2,1,0:T(2,128)(2,1)S(1)} %bitcast.280), channel_id=1, replica_groups=mesh['slot'=4,'seq'=2,'blk'=4] {'slot','blk'}, dimensions={0}, use_global_device_ids=true | all-gather | bytes 4352 | tf_op jit(solution)/shard_map/all_gather | solution.py:196
  475.9 45.5 %collective-permute-done.7 = bf16[128,4096]{1,0:T(8,128)(2,1)S(1)} collective-permute-done((bf16[128,4096]{1,0:T(8,128)(2,1)S(1)}, bf16[128,4096]{1,0:T(8,128)(2,1)S(1)}, u32[]{:S(2)}, u32[]{:S(2)}) %collective-permute-start.7) | collective-permute-done | bytes 1048608 | tf_op jit(solution)/shard_map/ppermute | solution.py:18
  522.4 49.0 %collective-permute-done.8 = bf16[128,4096]{1,0:T(8,128)(2,1)S(1)} collective-permute-done((bf16[128,4096]{1,0:T(8,128)(2,1)S(1)}, bf16[128,4096]{1,0:T(8,128)(2,1)S(1)}, u32[]{:S(2)}, u32[]{:S(2)}) %collective-permute-start.8) | collective-permute-done | bytes 1048608 | tf_op jit(solution)/shard_map/ppermute | solution.py:18
  574.4 42.5 %collective-permute-done.9 = bf16[128,4096]{1,0:T(8,128)(2,1)S(1)} collective-permute-done((bf16[128,4096]{1,0:T(8,128)(2,1)S(1)}, bf16[128,4096]{1,0:T(8,128)(2,1)S(1)}, u32[]{:S(2)}, u32[]{:S(2)}) %collective-permute-start.9) | collective-permute-done | bytes 1048608 | tf_op jit(solution)/shard_map/ppermute | solution.py:18
  617.0 51.1 %collective-permute-done.10 = bf16[128,4096]{1,0:T(8,128)(2,1)S(1)} collective-permute-done((bf16[128,4096]{1,0:T(8,128)(2,1)S(1)}, bf16[128,4096]{1,0:T(8,128)(2,1)S(1)}, u32[]{:S(2)}, u32[]{:S(2)}) %collective-permute-start.10) | collective-permute-done | bytes 1048608 | tf_op jit(solution)/shard_map/ppermute | solution.py:18
  671.2 60.8 %collective-permute-done.11 = bf16[128,4096]{1,0:T(8,128)(2,1)S(1)} collective-permute-done((bf16[128,4096]{1,0:T(8,128)(2,1)S(1)}, bf16[128,4096]{1,0:T(8,128)(2,1)S(1)}, u32[]{:S(2)}, u32[]{:S(2)}) %collective-permute-start.11) | collective-permute-done | bytes 1048608 | tf_op jit(solution)/shard_map/ppermute | solution.py:18
  741.5 35.0 %collective-permute-done.12 = bf16[128,4096]{1,0:T(8,128)(2,1)S(1)} collective-permute-done((bf16[128,4096]{1,0:T(8,128)(2,1)S(1)}, bf16[128,4096]{1,0:T(8,128)(2,1)S(1)}, u32[]{:S(2)}, u32[]{:S(2)}) %collective-permute-start.12) | collective-permute-done | bytes 1048608 | tf_op jit(solution)/shard_map/ppermute | solution.py:18
  777.6 50.1 %collective-permute-done.13 = bf16[128,4096]{1,0:T(8,128)(2,1)S(1)} collective-permute-done((bf16[128,4096]{1,0:T(8,128)(2,1)S(1)}, bf16[128,4096]{1,0:T(8,128)(2,1)S(1)}, u32[]{:S(2)}, u32[]{:S(2)}) %collective-permute-start.13) | collective-permute-done | bytes 1048608 | tf_op jit(solution)/shard_map/ppermute | solution.py:18
  828.7 50.0 %collective-permute-done.14 = bf16[128,4096]{1,0:T(8,128)(2,1)} collective-permute-done((bf16[128,4096]{1,0:T(8,128)(2,1)S(1)}, bf16[128,4096]{1,0:T(8,128)(2,1)}, u32[]{:S(2)}, u32[]{:S(2)}) %collective-permute-start.14) | collective-permute-done | bytes 1048608 | tf_op jit(solution)/shard_map/ppermute | solution.py:18
  878.7 45.2 %collective-permute-done.15 = bf16[128,4096]{1,0:T(8,128)(2,1)} collective-permute-done((bf16[128,4096]{1,0:T(8,128)(2,1)}, bf16[128,4096]{1,0:T(8,128)(2,1)}, u32[]{:S(2)}, u32[]{:S(2)}) %collective-permute-start.15) | collective-permute-done | bytes 1048608 | tf_op jit(solution)/shard_map/ppermute | solution.py:18
  935.9 38.2 %collective-permute-done.16 = bf16[128,4096]{1,0:T(8,128)(2,1)} collective-permute-done((bf16[128,4096]{1,0:T(8,128)(2,1)}, bf16[128,4096]{1,0:T(8,128)(2,1)}, u32[]{:S(2)}, u32[]{:S(2)}) %collective-permute-start.16) | collective-permute-done | bytes 1048608 | tf_op jit(solution)/shard_map/ppermute | solution.py:18
  977.3 53.7 %collective-permute-done.17 = bf16[128,4096]{1,0:T(8,128)(2,1)S(1)} collective-permute-done((bf16[128,4096]{1,0:T(8,128)(2,1)}, bf16[128,4096]{1,0:T(8,128)(2,1)S(1)}, u32[]{:S(2)}, u32[]{:S(2)}) %collective-permute-start.17) | collective-permute-done | bytes 1048608 | tf_op jit(solution)/shard_map/ppermute | solution.py:18
  1039.5 43.2 %collective-permute-done.18 = bf16[128,4096]{1,0:T(8,128)(2,1)S(1)} collective-permute-done((bf16[128,4096]{1,0:T(8,128)(2,1)S(1)}, bf16[128,4096]{1,0:T(8,128)(2,1)S(1)}, u32[]{:S(2)}, u32[]{:S(2)}) %collective-permute-start.18) | collective-permute-done | bytes 1048608 | tf_op jit(solution)/shard_map/ppermute | solution.py:18
  1391.0 42.1 %all-reduce.3 = (bf16[2048]{0:T(1024)(128)(2,1)S(1)}, bf16[2048]{0:T(1024)(128)(2,1)S(1)}) all-reduce(bf16[2048]{0:T(1024)(128)(2,1)S(1)} %get-tuple-element.228, bf16[2048]{0:T(1024)(128)(2,1)S(1)} %copy-done.67), channel_id=6, replica_groups=mesh['slot'=4,'seq'=2,'blk'=4] {'slot','blk'}, use_global_device_ids=true, to_apply=%region_18.19.clone | all-reduce | flops 4096 | bytes 16384
  1449.5 95.0 %reduce-scatter.24.cloned.1.call-done = bf16[128,1024]{1,0:T(8,128)(2,1)} async-done(((bf16[2048,1024]{1,0:T(8,128)(2,1)}), bf16[128,1024]{1,0:T(8,128)(2,1)}) %reduce-scatter.24.cloned.1.call-update) | async-done | bytes 262160 | tf_op jit(solution)/shard_map/reduce_scatter | solution.py:351
  1546.3 95.0 %reduce-scatter.22.cloned.1.call-done = bf16[128,1024]{1,0:T(8,128)(2,1)} async-done(((bf16[2048,1024]{1,0:T(8,128)(2,1)}), bf16[128,1024]{1,0:T(8,128)(2,1)}) %reduce-scatter.22.cloned.1.call-update) | async-done | bytes 262160 | tf_op jit(solution)/shard_map/reduce_scatter | solution.py:345
  1643.2 95.0 %reduce-scatter.20.cloned.1.call-done = bf16[128,1024]{1,0:T(8,128)(2,1)} async-done(((bf16[2048,1024]{1,0:T(8,128)(2,1)}), bf16[128,1024]{1,0:T(8,128)(2,1)}) %reduce-scatter.20.cloned.1.call-update) | async-done | bytes 262160 | tf_op jit(solution)/shard_map/reduce_scatter | solution.py:339
  1740.0 348.9 %reduce-scatter.28.cloned.1.call-done = bf16[128,4096]{1,0:T(8,128)(2,1)} async-done(((bf16[2048,4096]{1,0:T(8,128)(2,1)}), bf16[128,4096]{1,0:T(8,128)(2,1)}) %reduce-scatter.28.cloned.1.call-update) | async-done | bytes 1048592 | tf_op jit(solution)/shard_map/reduce_scatter | solution.py:138
  2091.6 348.4 %reduce-scatter.30.cloned.1.call-done = bf16[128,4096]{1,0:T(8,128)(2,1)} async-done(((bf16[2048,4096]{1,0:T(8,128)(2,1)}), bf16[128,4096]{1,0:T(8,128)(2,1)}) %reduce-scatter.30.cloned.1.call-update) | async-done | bytes 1048592 | tf_op jit(solution)/shard_map/reduce_scatter | solution.py:141
  2442.8 348.5 %reduce-scatter.32.cloned.1.call-done = bf16[128,4096]{1,0:T(8,128)(2,1)} async-done(((bf16[2048,4096]{1,0:T(8,128)(2,1)}), bf16[128,4096]{1,0:T(8,128)(2,1)}) %reduce-scatter.32.cloned.1.call-update) | async-done | bytes 1048592 | tf_op jit(solution)/shard_map/reduce_scatter | solution.py:144
  (386 shorter events, 540.2 us)
Async XLA Ops:
  7.2 51.2 %all-gather.13.cloned.1.call-start = ((), (), s32[]{:S(2)}) async-start(), calls=%async_computation.11 | async-start | bytes 1572864 | tf_op jit(solution)/shard_map/all_gather | solution.py:209
  52.9 85.3 %all-gather.15.cloned.1.call-start = ((), (), s32[]{:S(2)}) async-start(), calls=%async_computation.12 | async-start | bytes 4456448 | tf_op jit(solution)/shard_map/all_gather | solution.py:197
  53.7 161.9 %all-gather.17.cloned.1.call-start = ((), (), s32[]{:S(2)}) async-start(), calls=%async_computation.13 | async-start | bytes 4456448 | tf_op jit(solution)/shard_map/all_gather | solution.py:198
  54.4 239.9 %all-gather.19.cloned.1.call-start = ((), (), s32[]{:S(2)}) async-start(), calls=%async_computation.14 | async-start | bytes 4456448 | tf_op jit(solution)/shard_map/all_gather | solution.py:199
  55.0 345.5 %all-gather.21.cloned.1.call-start = ((), (), s32[]{:S(2)}) async-start(), calls=%async_computation.15 | async-start | bytes 4456448 | tf_op jit(solution)/shard_map/all_gather | solution.py:200
  55.6 390.7 %reduce-scatter.12.cloned.1.call-start = ((), (), s32[]{:S(2)}) async-start(), calls=%async_computation.16 | async-start | bytes 1572864 | tf_op jit(solution)/shard_map/reduce_scatter | solution.py:244
  219.9 84.1 %collective-permute-start = (bf16[256,16,64]{0,2,1:T(8,128)(2,1)S(1)}, bf16[256,16,64]{0,2,1:T(8,128)(2,1)S(1)}, u32[]{:S(2)}, u32[]{:S(2)}) collective-permute-start(bf16[256,16,64]{0,2,1:T(8,128)(2,1)S(1)} %pad_maximum_fusion.1), channel_id=1, source_target_pairs={{0,1},{1,2},{2,3},{4,5},{5,6},{6,7},{8,9},{9,10},{10,11},{12,13},{... | collective-permute-start | bytes 1572872 | tf_op jit(solution)/shard_map/ppermute | solution.py:26
  405.7 716.1 %all-gather.23.cloned.1.call-start = ((), (), s32[]{:S(2)}) async-start(), calls=%async_computation.17 | async-start | bytes 1572864 | tf_op jit(solution)/shard_map/all_gather | solution.py:252
  449.6 672.2 %all-gather.25.cloned.1.call-start = ((), (), s32[]{:S(2)}) async-start(), calls=%async_computation.18 | async-start | bytes 17825792 | tf_op jit(solution)/shard_map/all_gather | solution.py:202
  450.4 684.1 %all-gather.29.cloned.1.call-start = ((), (), s32[]{:S(2)}) async-start(), calls=%async_computation.21 | async-start | bytes 1572864 | tf_op jit(solution)/shard_map/all_gather | solution.py:265
  451.5 683.0 %all-gather.27.cloned.1.call-start = ((), (), s32[]{:S(2)}) async-start(), calls=%async_computation.19 | async-start | bytes 17825792 | tf_op jit(solution)/shard_map/all_gather | solution.py:203
  452.1 737.2 %reduce-scatter.16.cloned.1.call-start = ((), (), s32[]{:S(2)}) async-start(), calls=%async_computation.22 | async-start | bytes 1572864 | tf_op jit(solution)/shard_map/reduce_scatter | solution.py:274
  668.0 63.9 %collective-permute-start.11 = (bf16[128,4096]{1,0:T(8,128)(2,1)S(1)}, bf16[128,4096]{1,0:T(8,128)(2,1)S(1)}, u32[]{:S(2)}, u32[]{:S(2)}) collective-permute-start(bf16[128,4096]{1,0:T(8,128)(2,1)S(1)} %collective-permute-done.10), channel_id=1, source_target_pairs={{0,1},{1,2},{2,3},{3,8},{8,9},{9,10},{10,11},{11,16},{16,17},{17,1... | collective-permute-start | bytes 3145736 | tf_op jit(solution)/shard_map/ppermute | solution.py:18
  974.1 56.9 %collective-permute-start.17 = (bf16[128,4096]{1,0:T(8,128)(2,1)}, bf16[128,4096]{1,0:T(8,128)(2,1)S(1)}, u32[]{:S(2)}, u32[]{:S(2)}) collective-permute-start(bf16[128,4096]{1,0:T(8,128)(2,1)} %collective-permute-done.16), channel_id=1, source_target_pairs={{0,1},{1,2},{2,3},{3,8},{8,9},{9,10},{10,11},{11,16},{16,17},{17,1... | collective-permute-start | bytes 3145736 | tf_op jit(solution)/shard_map/ppermute | solution.py:18
  1031.0 51.8 %collective-permute-start.18 = (bf16[128,4096]{1,0:T(8,128)(2,1)S(1)}, bf16[128,4096]{1,0:T(8,128)(2,1)S(1)}, u32[]{:S(2)}, u32[]{:S(2)}) collective-permute-start(bf16[128,4096]{1,0:T(8,128)(2,1)S(1)} %collective-permute-done.17), channel_id=1, source_target_pairs={{0,1},{1,2},{2,3},{3,8},{8,9},{9,10},{10,11},{11,16},{16,17},{17,1... | collective-permute-start | bytes 3145736 | tf_op jit(solution)/shard_map/ppermute | solution.py:18
  1194.3 195.1 %reduce-scatter.18.cloned.1.call-start = ((), (), s32[]{:S(2)}) async-start(), calls=%async_computation.24 | async-start | bytes 1572864 | tf_op jit(solution)/shard_map/reduce_scatter | solution.py:324
  1326.0 110.1 %reduce-scatter.14.cloned.1.call-start = ((), (), s32[]{:S(2)}) async-start(), calls=%async_computation.20 | async-start | bytes 1572864 | tf_op jit(solution)/shard_map/reduce_scatter | solution.py:257
  1338.4 109.3 %reduce-scatter.26.cloned.1.call-start = ((), (), s32[]{:S(2)}) async-start(), calls=%async_computation.28 | async-start | bytes 4456448 | tf_op jit(solution)/shard_map/reduce_scatter | solution.py:357
  1343.3 201.2 %reduce-scatter.24.cloned.1.call-start = ((), (), s32[]{:S(2)}) async-start(), calls=%async_computation.27 | async-start | bytes 4456448 | tf_op jit(solution)/shard_map/reduce_scatter | solution.py:351
  1347.8 293.6 %reduce-scatter.22.cloned.1.call-start = ((), (), s32[]{:S(2)}) async-start(), calls=%async_computation.26 | async-start | bytes 4456448 | tf_op jit(solution)/shard_map/reduce_scatter | solution.py:345
  1351.2 386.9 %reduce-scatter.20.cloned.1.call-start = ((), (), s32[]{:S(2)}) async-start(), calls=%async_computation.25 | async-start | bytes 4456448 | tf_op jit(solution)/shard_map/reduce_scatter | solution.py:339
  1355.6 733.3 %reduce-scatter.28.cloned.1.call-start = ((), (), s32[]{:S(2)}) async-start(), calls=%async_computation.29 | async-start | bytes 17825792 | tf_op jit(solution)/shard_map/reduce_scatter | solution.py:138
  1366.7 1073.3 %reduce-scatter.30.cloned.1.call-start = ((), (), s32[]{:S(2)}) async-start(), calls=%async_computation.30 | async-start | bytes 17825792 | tf_op jit(solution)/shard_map/reduce_scatter | solution.py:141
  1376.5 1414.8 %reduce-scatter.32.cloned.1.call-start = ((), (), s32[]{:S(2)}) async-start(), calls=%async_computation.31 | async-start | bytes 17825792 | tf_op jit(solution)/shard_map/reduce_scatter | solution.py:144
  (110 other events, 3264.8 us)
Sparse Core Ops, SparseCore 0:
  53.0 5.3 all-gather.12
  61.1 77.0 all-gather.14
  141.0 74.4 all-gather.16
  218.1 76.0 all-gather.18
  296.9 100.4 all-gather.20
  405.9 9.3 reduce-scatter.11
  449.8 6.2 all-gather.22
  459.2 293.3 all-gather.24
  754.8 8.4 all-gather.28
  766.3 315.7 all-gather.26
  1179.9 9.3 reduce-scatter.15
  1194.4 10.1 all-gather.30
  1326.1 6.8 reduce-scatter.17
  1338.5 6.8 reduce-scatter.13
  1347.5 100.1 reduce-scatter.25
  1449.9 94.6 reduce-scatter.23
  1546.7 94.6 reduce-scatter.21
  1643.5 94.6 reduce-scatter.19
  1740.5 348.3 reduce-scatter.27
  2091.0 348.9 reduce-scatter.29
  2442.3 348.9 reduce-scatter.31
